TPU v7x, 32 devices: a whole 2x2x4 slice. The times are simulated.
32 devices in a mesh: dp: 4 (over y, core), row: 2 (over x), col: 4 (over z).
Axes of the slice: x: 2, y: 2, z: 4, core: 2. Of those that a mesh axis runs over, the one named last changes fastest.
Arguments:
- block_in: bfloat16 [2048, 1024], P(('dp', 'row'), 'col'), may hold values from -6 to 6
- cotangent: bfloat16 [2048, 1024], P(('dp', 'row'), 'col'), may hold values from -6 to 6
- segments: int32 [2048], P('dp'), may hold values from 0 to 18, as said below
- positions: int32 [2048], P('dp'), may hold values from 0 to 511, as said below
- attn_gain: float32 [1024], P('col'), may hold values from 0.5 to 1.5
- attn_shift: float32 [1024], P('col'), may hold values from -1.5 to 1.5
- mlp_gain: float32 [1024], P('col'), may hold values from 0.5 to 1.5
- mlp_shift: float32 [1024], P('col'), may hold values from -1.5 to 1.5
- qkv_weight: bfloat16 [1024, 3072], P('col', 'row'), may hold values from -0.1875 to 0.1875
- qkv_bias: float32 [3072], P(('row', 'col')), may hold values from -2.5 to 2.5
- out_weight: bfloat16 [1024, 1024], P('row', 'col'), may hold values from -1.5 to 1.5
- out_bias: float32 [1024], P('col'), may hold values from -2.5 to 2.5
- up_weight: bfloat16 [1024, 4096], P('col', 'row'), may hold values from -0.1875 to 0.1875
- up_bias: float32 [4096], P(('row', 'col')), may hold values from -2.5 to 2.5
- down_weight: bfloat16 [4096, 1024], P('row', 'col'), may hold values from -0.09375 to 0.09375
- down_bias: float32 [1024], P('col'), may hold values from -2.5 to 2.5
Outputs:
- block_out: bfloat16 [2048, 1024], P(('dp', 'row'), 'col')
- grad_in: bfloat16 [2048, 1024], P(('dp', 'row'), 'col')
- grad_qkv_weight: float32 [1024, 3072], P('col', 'row')
- grad_qkv_bias: float32 [3072], P(('row', 'col'))
- grad_out_weight: float32 [1024, 1024], P('row', 'col')
- grad_out_bias: float32 [1024], P('col')
- grad_up_weight: float32 [1024, 4096], P('col', 'row')
- grad_up_bias: float32 [4096], P(('row', 'col'))
- grad_down_weight: float32 [4096, 1024], P('row', 'col')
- grad_down_bias: float32 [1024], P('col')
- grad_attn_gain: float32 [1024], P('col')
- grad_attn_shift: float32 [1024], P('col')
- grad_mlp_gain: float32 [1024], P('col')
- grad_mlp_shift: float32 [1024], P('col')
Inputs may be any that keep to these rules, and one draw needn't show every extreme that they name: segments never fall along the tokens, and every packed sequence of 512 tokens begins a new segment. `positions`: a token's position is the number of tokens before it in its segment.
All inputs are finite; a program needn't handle non-finite values.
Results may differ from a plain program's by a relative error of at most 0.011.
Values may be sent and summed in bfloat16 or wider, within the bound.
No kernel may reach another device: no remote copies, remote signals or barrier semaphores. Data moves between devices by JAX's collectives and lax.ppermute only.
A program may use at most 64 MiB of HBM per device.

v0:
```python
import math
import jax
import jax.numpy as jnp
from jax import lax
from jax.sharding import PartitionSpec as P

D = 1024
HD = 64
ROT = 16
EPS = 1e-05
NEG = -1e30


def rotary_tables(positions, rot_dims):
    half_dims = rot_dims // 2
    exponent = jnp.arange(half_dims, dtype=jnp.float32) * (2.0 / rot_dims)
    inverse = jnp.power(10000.0, -exponent)
    angles = positions.astype(jnp.float32)[:, None] * inverse[None, :]
    cosine = jnp.cos(angles)
    sine_tab = jnp.sin(angles)
    return (jnp.concatenate([cosine, cosine], 1), jnp.concatenate([sine_tab, sine_tab], 1))


def rotate_fwd(values, cosine, sine_tab):
    rot_dims = cosine.shape[1]
    half_dims = rot_dims // 2
    front = values[..., :rot_dims]
    turned = jnp.concatenate([-front[..., half_dims:], front[..., :half_dims]], -1)
    moved = front * cosine[:, None, :] + turned * sine_tab[:, None, :]
    return jnp.concatenate([moved, values[..., rot_dims:]], -1)


def rotate_back(grads, cosine, sine_tab):
    rot_dims = cosine.shape[1]
    half_dims = rot_dims // 2
    front = grads[..., :rot_dims]
    scaled = front * sine_tab[:, None, :]
    turned = jnp.concatenate([scaled[..., half_dims:], -scaled[..., :half_dims]], -1)
    moved = front * cosine[:, None, :] + turned
    return jnp.concatenate([moved, grads[..., rot_dims:]], -1)


def score_block(queries, keys_b, segments, start, width):
    length = keys_b.shape[0]
    raw = jnp.einsum("qhd,khd->hqk", queries, keys_b, preferred_element_type=jnp.float32) * (
        1.0 / math.sqrt(HD)
    )
    query_pos = start + jnp.arange(width, dtype=jnp.int32)
    key_pos = jnp.arange(length, dtype=jnp.int32)
    allowed = (key_pos[None, :] <= query_pos[:, None]) & (segments[None, :] == segments[:, None])
    return (jnp.where(allowed[None], raw, NEG), allowed)


def attend(queries, keys_b, values, segments):
    length, heads_here, head_dim = queries.shape
    width = min(512, length)
    count = length // width

    def one_block(index):
        start = index * width
        scores, allowed = score_block(queries, keys_b, segments, start, width)
        top = jnp.max(scores, -1, keepdims=True)
        expo = jnp.exp(scores - top)
        total = jnp.sum(expo, -1, keepdims=True)
        weights = (expo / total).astype(jnp.bfloat16)
        attended = jnp.einsum("hqk,khd->qhd", weights, values, preferred_element_type=jnp.float32)
        return (attended, (top + jnp.log(total))[..., 0])

    attended, log_total = lax.map(one_block, jnp.arange(count, dtype=jnp.int32))
    attended = attended.reshape(length, heads_here, head_dim)
    log_total = jnp.transpose(log_total, (1, 0, 2)).reshape(heads_here, length)
    return (attended, log_total)


def attend_back(queries, keys_b, values, grad_att, log_total, segments):
    length, heads_here, head_dim = queries.shape
    width = min(512, length)
    count = length // width
    scale = 1.0 / math.sqrt(HD)

    def one_block(carry, index):
        grad_keys, grad_values = carry
        start = index * width
        scores, allowed = score_block(queries, keys_b, segments, start, width)
        probs = jnp.where(allowed[None], jnp.exp(scores - log_total[..., None]), 0.0)
        probs_b = probs.astype(jnp.bfloat16)
        grad_values = grad_values + jnp.einsum(
            "hqk,qhd->khd", probs_b, grad_att, preferred_element_type=jnp.float32
        )
        grad_probs = jnp.einsum(
            "qhd,khd->hqk", grad_att, values, preferred_element_type=jnp.float32
        )
        delta = jnp.sum(probs * grad_probs, -1, keepdims=True)
        grad_scores = (probs * (grad_probs - delta) * scale).astype(jnp.bfloat16)
        grad_part = jnp.einsum(
            "hqk,khd->qhd", grad_scores, keys_b, preferred_element_type=jnp.float32
        )
        grad_keys = grad_keys + jnp.einsum(
            "hqk,qhd->khd", grad_scores, queries, preferred_element_type=jnp.float32
        )
        return ((grad_keys, grad_values), grad_part)

    zeros_kv = jnp.zeros((length, heads_here, head_dim), jnp.float32)
    (grad_keys, grad_values), grad_queries = lax.scan(
        one_block, (zeros_kv, zeros_kv), jnp.arange(count, dtype=jnp.int32)
    )
    return (grad_queries.reshape(length, heads_here, head_dim), grad_keys, grad_values)


def normal_cdf(values):
    return 0.5 * (1.0 + lax.erf(values * (1.0 / math.sqrt(2.0))))


def gelu_slope(values):
    return normal_cdf(values) + values * jnp.exp(-0.5 * values * values) * (
        1.0 / math.sqrt(2.0 * math.pi)
    )


def shards(
    block_in,
    cotangent,
    segments,
    positions,
    attn_gain,
    attn_shift,
    mlp_gain,
    mlp_shift,
    qkv_weight,
    qkv_bias,
    out_weight,
    out_bias,
    up_weight,
    up_bias,
    down_weight,
    down_bias,
):
    col_count = lax.axis_size("col")
    local_rows, local_width = block_in.shape
    length = segments.shape[0]
    qkv_share = qkv_weight.shape[1] // col_count
    up_share = up_weight.shape[1] // col_count
    heads_here = qkv_share // (3 * HD)
    att_width = heads_here * HD
    residual = block_in.astype(jnp.float32)
    totals = lax.psum((jnp.sum(residual, 1), jnp.sum(residual * residual, 1)), "col")
    average = totals[0][:, None] / D
    spread = totals[1][:, None] / D - average * average
    inv_std = lax.rsqrt(spread + EPS)
    normal = (residual - average) * inv_std
    normed = jnp.stack([normal * attn_gain + attn_shift, normal * mlp_gain + mlp_shift]).astype(
        jnp.bfloat16
    )
    normed_rows = lax.all_gather(normed, "row", axis=1, tiled=True)
    start = jnp.int32(0)
    blocks = []
    for offset in range(length * lax.axis_size("col") // length):
        piece_idx = start // length + offset
        qkv_part = lax.dynamic_slice_in_dim(qkv_weight, piece_idx * qkv_share, qkv_share, 1)
        up_part = lax.dynamic_slice_in_dim(up_weight, piece_idx * up_share, up_share, 1)
        blocks.append(
            jnp.concatenate(
                [
                    jnp.dot(normed_rows[0], qkv_part, preferred_element_type=jnp.float32),
                    jnp.dot(normed_rows[1], up_part, preferred_element_type=jnp.float32),
                ],
                1,
            )
        )
    first = lax.psum_scatter(jnp.concatenate(blocks, 0), "col", scatter_dimension=0, tiled=True)
    merged = first[:, :qkv_share] + qkv_bias
    up_proj = first[:, qkv_share:] + up_bias
    packed = merged.reshape(length, heads_here, 3, HD)
    cosine, sine_tab = rotary_tables(positions, ROT)
    queries = rotate_fwd(packed[:, :, 0], cosine, sine_tab).astype(jnp.bfloat16)
    keys_b = rotate_fwd(packed[:, :, 1], cosine, sine_tab).astype(jnp.bfloat16)
    values = packed[:, :, 2].astype(jnp.bfloat16)
    attended, log_total = attend(queries, keys_b, values, segments)
    attended = attended.reshape(length, att_width).astype(jnp.bfloat16)
    activated = (up_proj * normal_cdf(up_proj)).astype(jnp.bfloat16)
    mixed_cols = lax.all_gather(
        jnp.concatenate([attended, activated], 1), "col", axis=1, tiled=True
    )
    joined_grid = jnp.concatenate(
        [
            out_weight.reshape(col_count, att_width, local_width),
            down_weight.reshape(col_count, up_share, local_width),
        ],
        1,
    )
    joined = joined_grid.reshape(col_count * (att_width + up_share), local_width)
    mixed = lax.psum_scatter(
        jnp.dot(mixed_cols, joined, preferred_element_type=jnp.float32).astype(jnp.bfloat16),
        "row",
        scatter_dimension=0,
        tiled=True,
    ).astype(jnp.float32)
    block_out = (mixed + out_bias + down_bias + residual).astype(jnp.bfloat16)
    cot_rows = lax.all_gather(cotangent, "row", axis=0, tiled=True)
    grad_bias_out = jnp.sum(cot_rows.astype(jnp.float32), 0)
    grad_joined = jnp.dot(mixed_cols.T, cot_rows, preferred_element_type=jnp.float32)
    grad_joined = grad_joined.reshape(col_count, att_width + up_share, local_width)
    grad_out_w = grad_joined[:, :att_width].reshape(col_count * att_width, local_width)
    grad_down_w = grad_joined[:, att_width:].reshape(col_count * up_share, local_width)
    own_rows = lax.all_to_all(joined_grid, "col", split_axis=0, concat_axis=2, tiled=True)[0]
    cot_full = lax.all_gather(cot_rows, "col", axis=1, tiled=True)
    back = jnp.einsum("td,fd->tf", cot_full, own_rows, preferred_element_type=jnp.float32)
    grad_att = back[:, :att_width].astype(jnp.bfloat16).reshape(length, heads_here, HD)
    grad_up = back[:, att_width:] * gelu_slope(up_proj)
    grad_queries, grad_keys, grad_values = attend_back(
        queries, keys_b, values, grad_att, log_total, segments
    )
    grad_queries = rotate_back(grad_queries, cosine, sine_tab)
    grad_keys = rotate_back(grad_keys, cosine, sine_tab)
    grad_merged = jnp.stack([grad_queries, grad_keys, grad_values], 2).reshape(length, qkv_share)
    grad_qkv_b = jnp.sum(grad_merged, 0)
    grad_up_b = jnp.sum(grad_up, 0)
    first_back = jnp.concatenate(
        [grad_merged.astype(jnp.bfloat16), grad_up.astype(jnp.bfloat16)], 1
    )
    first_cols = lax.all_gather(first_back, "col", axis=1, tiled=True)
    split_cols = first_cols.reshape(length, col_count, qkv_share + up_share)
    merged_cols = split_cols[:, :, :qkv_share].reshape(length, col_count * qkv_share)
    up_cols = split_cols[:, :, qkv_share:].reshape(length, col_count * up_share)
    grad_qkv_w = jnp.dot(normed_rows[0].T, merged_cols, preferred_element_type=jnp.float32)
    grad_up_w = jnp.dot(normed_rows[1].T, up_cols, preferred_element_type=jnp.float32)
    up_part = up_cols
    grad_normed = lax.psum_scatter(
        jnp.stack(
            [
                jnp.dot(merged_cols, qkv_weight.T, preferred_element_type=jnp.float32),
                jnp.dot(up_part, up_weight.T, preferred_element_type=jnp.float32),
            ],
            1,
        ).astype(jnp.bfloat16),
        "row",
        scatter_dimension=0,
        tiled=True,
    ).astype(jnp.float32)
    grad_attn_in = grad_normed[:, 0]
    grad_mlp_in = grad_normed[:, 1]
    grad_normal = grad_attn_in * attn_gain + grad_mlp_in * mlp_gain
    grad_totals = lax.psum((jnp.sum(grad_normal, 1), jnp.sum(grad_normal * normal, 1)), "col")
    grad_x = cotangent.astype(jnp.float32) + inv_std * (
        grad_normal - grad_totals[0][:, None] / D - normal * (grad_totals[1][:, None] / D)
    )
    norm_params = lax.psum(
        (
            jnp.sum(grad_attn_in * normal, 0),
            jnp.sum(grad_attn_in, 0),
            jnp.sum(grad_mlp_in * normal, 0),
            jnp.sum(grad_mlp_in, 0),
        ),
        ("dp", "row"),
    )
    summed = (
        lax.psum(grad_qkv_w.astype(jnp.bfloat16), "dp").astype(jnp.float32),
        lax.psum(grad_qkv_b.astype(jnp.bfloat16), "dp").astype(jnp.float32),
        lax.psum(grad_out_w.astype(jnp.bfloat16), "dp").astype(jnp.float32),
        lax.psum(grad_bias_out.astype(jnp.bfloat16), "dp").astype(jnp.float32),
        lax.psum(grad_up_w.astype(jnp.bfloat16), "dp").astype(jnp.float32),
        lax.psum(grad_up_b.astype(jnp.bfloat16), "dp").astype(jnp.float32),
        lax.psum(grad_down_w.astype(jnp.bfloat16), "dp").astype(jnp.float32),
    )
    return (
        block_out,
        grad_x.astype(jnp.bfloat16),
        summed[0],
        summed[1],
        summed[2],
        summed[3],
        summed[4],
        summed[5],
        summed[6],
        summed[3],
        norm_params[0],
        norm_params[1],
        norm_params[2],
        norm_params[3],
    )


def solution(mesh):
    return jax.shard_map(
        shards,
        mesh=mesh,
        in_specs=(
            P(("dp", "row"), "col"),
            P(("dp", "row"), "col"),
            P("dp"),
            P("dp"),
            P("col"),
            P("col"),
            P("col"),
            P("col"),
            P("col", "row"),
            P(("row", "col")),
            P("row", "col"),
            P("col"),
            P("col", "row"),
            P(("row", "col")),
            P("row", "col"),
            P("col"),
        ),
        out_specs=(
            P(("dp", "row"), "col"),
            P(("dp", "row"), "col"),
            P("col", "row"),
            P(("row", "col")),
            P("row", "col"),
            P("col"),
            P("col", "row"),
            P(("row", "col")),
            P("row", "col"),
            P("col"),
            P("col"),
            P("col"),
            P("col"),
            P("col"),
        ),
        check_vma=False,
    )
```

profile of v0, /device:TPU:0, one launch (start us, length us, event | category | flops | bytes accessed | tf_op | source)
XLA Modules:
  0.0 464.6 jit_solution(14196637380774124360)
XLA Ops:
  7.2 9.1 %all_gather.17 = bf16[512,256]{1,0:T(8,128)(2,1)} all-gather(bf16[256,256]{1,0:T(8,128)(2,1)} %param.17), channel_id=1, replica_groups=mesh['dp'=4,'row'=2,'col'=4] {'row'}, dimensions={0}, use_global_device_ids=true | all-gather | bytes 393216 | tf_op jit(solution)/shard_map/all_gather | solution.py:199
  16.4 1.1 convert_reduce_fusion
  17.5 12.1 %all-reduce.2 = (f32[256]{0:T(256)S(1)}, f32[256]{0:T(256)S(1)}) all-reduce(f32[256]{0:T(256)S(1)} %get-tuple-element.74, f32[256]{0:T(256)S(1)} %get-tuple-element.73), channel_id=1, replica_groups=mesh['dp'=4,'row'=2,'col'=4] {'col'}, use_global_device_ids=true, to_apply=%region_3.0 | all-reduce | flops 512 | bytes 4096 | tf_op jit(solution)/shard_map/psum | solution.py:146
  29.6 1.1 fusion.69
  30.7 7.2 %all_gather.15 = bf16[2,512,256]{2,1,0:T(8,128)(2,1)S(1)} all-gather(bf16[2,256,256]{2,1,0:T(8,128)(2,1)S(1)} %pad_maximum_fusion.5), channel_id=1, replica_groups=mesh['dp'=4,'row'=2,'col'=4] {'row'}, dimensions={1}, use_global_device_ids=true | all-gather | bytes 786432 | tf_op jit(solution)/shard_map/all_gather | solution.py:154
  37.9 0.3 fusion.59
  38.9 0.3 fusion.51
  39.5 0.4 fusion.53
  39.9 0.4 fusion.55
  40.2 0.4 fusion.57
  40.6 8.6 %maximum_maximum_fusion = f32[2048,896]{0,1:T(8,128)} fusion(f32[512,512]{0,1:T(8,128)S(1)} %fusion.51, f32[512,384]{0,1:T(8,128)S(1)} %fusion.59, f32[512,512]{0,1:T(8,128)S(1)} %fusion.53, f32[512,384]{0,1:T(8,128)S(1)} %fusion.61, f32[512,512]{0,1:T(8,128)S(1)} %fusion.55, f32[512,384]{0,1:T(8,128)S(1)} %fusion.63, f32[512,512]{0,1:T(8,128)S(1)} %fusion.57, ...), kind=kLoop, calls=%fused_computation.1 | loop fusion | flops 12845056 | bytes 14680064 | tf_op jit(solution)/shard_map/concatenate | solution.py:170
  49.3 1.2 copy-done.9
  50.5 1.1 pad_maximum_fusion
  51.6 3.6 all-to-all-start
  55.7 0.9 fusion.27
  56.6 65.1 %all-to-all-done = bf16[4,640,256]{2,1,0:T(8,128)(2,1)S(1)} async-done(((bf16[4,640,256]{2,1,0:T(8,128)(2,1)}), bf16[4,640,256]{2,1,0:T(8,128)(2,1)S(1)}, u32[]{:S(2)}, u32[]{:S(2)}) %all-to-all-start) | async-done | bytes 1310752 | tf_op jit(solution)/shard_map/all_to_all | solution.py:205
  121.7 0.7 copy.59
  122.5 2.2 convolution_bitcast_fusion
  124.7 1.0 copy-done.6
  125.7 69.3 %reduce-scatter.4.cloned.1.call-done = f32[512,896]{0,1:T(8,128)} async-done(((f32[2048,896]{0,1:T(8,128)}), f32[512,896]{0,1:T(8,128)}) %reduce-scatter.4.cloned.1.call-update) | async-done | bytes 1835024 | tf_op jit(solution)/shard_map/reduce_scatter | solution.py:170
  195.0 1.2 slice_add_fusion.1
  196.5 0.6 fusion.94
  197.5 0.9 log_add_fusion
  198.5 0.5 fusion.74
  199.0 4.7 %fusion.12 = f32[512,2,64]{0,2,1:T(8,128)} fusion(f32[2,512,512]{1,2,0:T(8,128)S(1)} %fusion.74, f32[2,512,512]{1,2,0:T(8,128)} %copy-done.4, f32[2,512]{1,0:T(2,128)} %log_add_fusion, pred[512,512]{0,1:T(8,128)(4,1)} %fusion.27, bf16[512,2,48]{0,2,1:T(8,128)(2,1)} %copy-done.26, bf16[512,2,16]{0,2,1:T(8,128)(2,1)} %copy-done.29), kind=kOutput, calls=%fused_computation.22 | convolution fusion | flops 72091136 | bytes 4853760 | tf_op jit(solution)/shard_map/while/body/eval_jaxpr/hqk,khd->qhd/dot_general | solution.py:95
  203.6 4.7 %fusion.15 = f32[512,2,64]{0,2,1:T(8,128)} fusion(f32[2,512,512]{1,2,0:T(8,128)S(1)} %fusion.74, f32[2,512,512]{1,2,0:T(8,128)} %copy-done.4, f32[2,512]{1,0:T(2,128)} %log_add_fusion, pred[512,512]{0,1:T(8,128)(4,1)} %fusion.27, bf16[512,2,48]{0,2,1:T(8,128)(2,1)} %copy-done.27, bf16[512,2,16]{0,2,1:T(8,128)(2,1)} %copy-done.28), kind=kOutput, calls=%fused_computation.23 | convolution fusion | flops 72091136 | bytes 4853760 | tf_op jit(solution)/shard_map/while/body/eval_jaxpr/hqk,qhd->khd/dot_general | solution.py:98
  208.3 1.0 slice_multiply_fusion.3
  209.3 2.2 convolution_bitcast_fusion.1
  211.8 0.5 copy-done.10
  212.3 0.8 copy-done.5
  213.1 0.4 copy-done.7
  213.5 0.7 fusion.88
  214.2 1.0 pad_maximum_fusion.1
  215.3 2.1 convolution_convert_fusion.6
  217.3 0.9 pad_maximum_fusion.3
  218.3 74.6 %all-gather.8.cloned.1.call-done = bf16[512,3584]{0,1:T(8,128)(2,1)} async-done(((bf16[512,896]{0,1:T(8,128)(2,1)}), bf16[512,3584]{0,1:T(8,128)(2,1)}) %all-gather.8.cloned.1.call-update) | async-done | bytes 3670032 | tf_op jit(solution)/shard_map/all_gather | solution.py:221
  292.9 1.7 slice.176
  294.6 1.6 slice.175
  296.2 0.6 fusion.11
  296.9 1.1 copy-done.13
  298.0 0.8 fusion.18
  298.8 0.8 pad_maximum_fusion.4
  299.7 48.5 %all-gather.4.cloned.1.call-done = bf16[512,2560]{0,1:T(8,128)(2,1)} async-done(((bf16[512,640]{0,1:T(8,128)(2,1)}), bf16[512,2560]{0,1:T(8,128)(2,1)}) %all-gather.4.cloned.1.call-update) | async-done | bytes 2621456 | tf_op jit(solution)/shard_map/all_gather | solution.py:181
  348.2 2.6 convolution_convert_fusion
  350.8 1.0 slice.180
  351.8 0.7 slice.179
  352.6 0.4 copy-done.1
  353.0 2.9 convolution_convert_fusion.3
  356.2 2.9 convolution_convert_fusion.2
  359.1 1.7 convolution_convert_fusion.1
  361.0 0.8 copy-done.11
  362.0 6.4 %all-reduce.3 = (bf16[384]{0:T(512)(128)(2,1)S(1)}, bf16[256]{0:T(256)(128)(2,1)S(1)}, bf16[512]{0:T(512)(128)(2,1)S(1)}) all-reduce(bf16[384]{0:T(512)(128)(2,1)S(1)} %convert_element_type.134, bf16[256]{0:T(256)(128)(2,1)S(1)} %reduce_sum.129, bf16[512]{0:T(512)(128)(2,1)S(1)} %get-tuple-element.90), channel_id=1, replica_groups=mesh['dp'=4,'row'=2,'col'=4] {'dp'}, use_global_device_ids=true, to_apply=%region_16.17 | all-reduce | flops 1152 | bytes 4608 | tf_op jit(solution)/shard_map/psum | solution.py:258
  368.4 0.6 convert_element_type.135
  369.0 0.6 convert_element_type.142
  369.6 1.0 convert_element_type.129
  370.9 14.2 %all-reduce = (f32[256]{0:T(256)}, f32[256]{0:T(256)}, f32[256]{0:T(256)}, f32[256]{0:T(256)}) all-reduce(f32[256]{0:T(256)S(1)} %get-tuple-element.71, f32[256]{0:T(256)S(1)} %get-tuple-element.68, f32[256]{0:T(256)S(1)} %get-tuple-element.72, f32[256]{0:T(256)S(1)} %get-tuple-element.57), channel_id=1, replica_groups=mesh['dp'=4,'row'=2,'col'=4] {'dp','row'}, use_global_device_ids=true, to_apply=%region_25.26 | all-reduce | flops 1024 | bytes 8192 | tf_op jit(solution)/shard_map/psum | solution.py:247
  385.1 9.7 %all-reduce.1 = (f32[256]{0:T(256)S(1)}, f32[256]{0:T(256)S(1)}) all-reduce(f32[256]{0:T(256)S(1)} %get-tuple-element.70, f32[256]{0:T(256)S(1)} %get-tuple-element.69), channel_id=1, replica_groups=mesh['dp'=4,'row'=2,'col'=4] {'col'}, use_global_device_ids=true, to_apply=%region_13.14 | all-reduce | flops 512 | bytes 4096 | tf_op jit(solution)/shard_map/psum | solution.py:243
  394.9 1.8 fusion.45
  396.7 54.0 %all-reduce.7.cloned.1.call-done = (bf16[256,1536]{1,0:T(8,128)(2,1)}, bf16[512,256]{1,0:T(8,128)(2,1)}, bf16[256,2048]{1,0:T(8,128)(2,1)}, bf16[2048,256]{1,0:T(8,128)(2,1)}) async-done(((bf16[256,1536]{1,0:T(8,128)(2,1)}, bf16[512,256]{1,0:T(8,128)(2,1)}, bf16[256,2048]{1,0:T(8,128)(2,1)}, bf16[2048,256]{1,0:T(8,128)(2,1)}), (bf16[256,1536]{1,0:T(8,128)(2,1)}, bf16[512,256]{1,0:T(8,128)(2,1)}, ...) | async-done | bytes 3145744 | tf_op jit(solution)/shard_map/psum | solution.py:257
  450.6 2.9 convert_element_type.140
  453.5 1.5 convert_element_type.144
  455.0 1.3 convert_element_type.132
  456.3 0.8 convert_element_type.137
  457.2 0.6 copy.84
  (125 shorter events, 3.6 us)
Async XLA Ops:
  7.2 30.7 %copy-start.14 = (bf16[256,1536]{1,0:T(8,128)(2,1)S(1)}, bf16[256,1536]{1,0:T(8,128)(2,1)}, u32[]{:S(2)}) copy-start(bf16[256,1536]{1,0:T(8,128)(2,1)} %param.24) | copy-start | bytes 2359300
  7.2 115.3 %all-gather.6.cloned.1.call-start = ((), (), s32[]{:S(2)}) async-start(), calls=%async_computation.7 | async-start | bytes 1310720 | tf_op jit(solution)/shard_map/all_gather | solution.py:206
  16.4 178.6 %reduce-scatter.4.cloned.1.call-start = ((), (), s32[]{:S(2)}) async-start(), calls=%async_computation.4 | async-start | bytes 9175040 | tf_op jit(solution)/shard_map/reduce_scatter | solution.py:170
  30.7 8.1 %copy-start.12 = (bf16[256,2048]{1,0:T(8,128)(2,1)S(1)}, bf16[256,2048]{1,0:T(8,128)(2,1)}, u32[]{:S(2)}) copy-start(bf16[256,2048]{1,0:T(8,128)(2,1)} %param.28) | copy-start | bytes 3145732
  49.2 1.2 copy-start.9
  49.2 1.3 copy-start.23
  50.5 5.0 %copy-start.35 = (s32[512]{0:T(512)S(1)}, s32[512]{0:T(512)}, u32[]{:S(2)}) copy-start(s32[512]{0:T(512)} %param.19) | copy-start | bytes 6148
  50.5 5.2 %copy-start.30 = (s32[512]{0:T(512)S(1)}, s32[512]{0:T(512)}, u32[]{:S(2)}) copy-start(s32[512]{0:T(512)} %param.18) | copy-start | bytes 6148
  51.6 70.1 %all-to-all-start = ((bf16[4,640,256]{2,1,0:T(8,128)(2,1)}), bf16[4,640,256]{2,1,0:T(8,128)(2,1)S(1)}, u32[]{:S(2)}, u32[]{:S(2)}) async-start(bf16[4,640,256]{2,1,0:T(8,128)(2,1)} %pad_maximum_fusion), calls=%async_computation.2 | async-start | bytes 2621440 | tf_op jit(solution)/shard_map/all_to_all | solution.py:205
  55.3 237.6 %all-gather.8.cloned.1.call-start = ((), (), s32[]{:S(2)}) async-start(), calls=%async_computation.8 | async-start | bytes 4587520 | tf_op jit(solution)/shard_map/all_gather | solution.py:221
  55.7 140.7 %copy-start.20 = (f32[512,16]{0,1:T(8,128)}, f32[512,16]{0,1:T(8,128)S(1)}, u32[]{:S(2)}) copy-start(f32[512,16]{0,1:T(8,128)S(1)} %get-tuple-element.123) | copy-start | bytes 98308
  55.7 140.7 %copy-start.21 = (f32[512,16]{0,1:T(8,128)}, f32[512,16]{0,1:T(8,128)S(1)}, u32[]{:S(2)}) copy-start(f32[512,16]{0,1:T(8,128)S(1)} %get-tuple-element.122) | copy-start | bytes 98308
  122.5 72.5 %copy-start.33 = (f32[384]{0:T(512)S(1)}, f32[384]{0:T(512)}, u32[]{:S(2)}) copy-start(f32[384]{0:T(512)} %param.25) | copy-start | bytes 4612
  124.7 1.1 copy-start.6
  125.7 70.8 %copy-start.25 = (pred[512,512]{0,1:T(8,128)(4,1)S(1)}, pred[512,512]{0,1:T(8,128)(4,1)}, u32[]{:S(2)}) copy-start(pred[512,512]{0,1:T(8,128)(4,1)} %fusion.27) | copy-start | bytes 786436
  196.4 1.1 copy-start.26
  196.4 1.1 copy-start.27
  196.5 1.0 copy-start.28
  196.5 1.0 copy-start.29
  197.2 1.3 copy-start.4
  208.3 3.3 copy-start.16
  208.3 3.3 copy-start.17
  208.3 3.3 copy-start.22
  208.3 3.3 slice-start
  209.3 2.4 slice-start.1
  211.5 0.7 copy-start.10
  211.5 1.6 copy-start.5
  211.5 2.0 copy-start.7
  211.6 1.9 copy-start.34
  215.2 133.0 %all-gather.4.cloned.1.call-start = ((), (), s32[]{:S(2)}) async-start(), calls=%async_computation.5 | async-start | bytes 3276800 | tf_op jit(solution)/shard_map/all_gather | solution.py:181
  218.2 151.4 %reduce-scatter.8.cloned.1.call-start = ((), (), s32[]{:S(2)}) async-start(), calls=%async_computation.9 | async-start | bytes 786432 | tf_op jit(solution)/shard_map/reduce_scatter | solution.py:228
  294.6 1.6 copy-start.15
  296.2 2.6 copy-start
  296.2 1.8 copy-start.13
  298.0 50.2 %copy-start.2 = (bf16[512,256]{1,0:T(8,128)(2,1)S(1)}, bf16[512,256]{1,0:T(8,128)(2,1)}, u32[]{:S(2)}) copy-start(bf16[512,256]{1,0:T(8,128)(2,1)} %all_gather.17) | copy-start | bytes 786436
  299.7 95.2 %reduce-scatter.6.cloned.1.call-start = ((), (), s32[]{:S(2)}) async-start(), calls=%async_computation.6 | async-start | bytes 393216 | tf_op jit(solution)/shard_map/reduce_scatter | solution.py:192
  350.8 2.2 copy-start.1
  355.9 94.7 %all-reduce.7.cloned.1.call-start = ((), (), s32[]{:S(2)}) async-start(), calls=%async_computation.10 | async-start | bytes 6291456 | tf_op jit(solution)/shard_map/psum | solution.py:257
  360.9 0.9 copy-start.11
  360.9 9.8 %copy-start.3 = (bf16[256,256]{1,0:T(8,128)(2,1)S(1)}, bf16[256,256]{1,0:T(8,128)(2,1)}, u32[]{:S(2)}) copy-start(bf16[256,256]{1,0:T(8,128)(2,1)} %param.16) | copy-start | bytes 393220
  360.9 9.8 %copy-start.31 = (f32[256]{0:T(256)S(1)}, f32[256]{0:T(256)}, u32[]{:S(2)}) copy-start(f32[256]{0:T(256)} %param.20) | copy-start | bytes 3076
  360.9 9.8 %copy-start.32 = (f32[256]{0:T(256)S(1)}, f32[256]{0:T(256)}, u32[]{:S(2)}) copy-start(f32[256]{0:T(256)} %param.22) | copy-start | bytes 3076
  360.9 34.0 %copy-start.19 = (bf16[256,256]{1,0:T(8,128)(2,1)S(1)}, bf16[256,256]{1,0:T(8,128)(2,1)}, u32[]{:S(2)}) copy-start(bf16[256,256]{1,0:T(8,128)(2,1)} %param.17) | copy-start | bytes 393220
  360.9 34.0 %copy-start.36 = (f32[256]{0:T(256)S(1)}, f32[256]{0:T(256)}, u32[]{:S(2)}) copy-start(f32[256]{0:T(256)} %param.31) | copy-start | bytes 3076
  360.9 34.0 %copy-start.37 = (f32[256]{0:T(256)S(1)}, f32[256]{0:T(256)}, u32[]{:S(2)}) copy-start(f32[256]{0:T(256)} %param.27) | copy-start | bytes 3076
  369.6 87.6 %copy-start.38 = (f32[256]{0:T(256)}, f32[256]{0:T(256)S(1)}, u32[]{:S(2)}) copy-start(f32[256]{0:T(256)S(1)} %convert_element_type.138) | copy-start | bytes 3076
  450.6 2.9 copy-start.8
  453.5 1.5 copy-start.18
  453.5 2.8 copy-start.24
Sparse Core Ops, SparseCore 0:
  16.5 30.1 all-gather.5
  49.4 145.5 reduce-scatter.3
  215.3 77.4 all-gather.7
  294.9 53.2 all-gather.3
  350.9 13.3 reduce-scatter.7
  366.4 11.9 reduce-scatter.5
  382.1 68.5 all-reduce.6
where the time goes:
time: 465 us
  waiting for transfers between devices  312 us (67%)
  blocking collectives  58.6 us (13%)
  other arithmetic  31 us (7%)
  matrix products  31 us (7%)
  between operations  14.8 us (3%)
  local copies, waits for them, and re-layouts  13.2 us (3%)
    all_gather x1, waiting for transfers between devices, shards(): first_cols = lax.all_gather(first_back, 'col', axis=1, tiled=True)  74.6 us
    reduce_scatter x1, waiting for transfers between devices, shards(): lax.psum_scatter(jnp.concatenate(blocks, 0), 'col', scatter_dimension=0,...  69.3 us
    all_to_all x1, waiting for transfers between devices, shards(): lax.all_to_all(joined_grid, 'col', split_axis=0, concat_axis=2, tiled=True)  65.1 us
    psum x1, waiting for transfers between devices, shards(): lax.psum(grad_qkv_w.astype(jnp.bfloat16), 'dp').astype(jnp.float32)  54 us
    all_gather x1, waiting for transfers between devices, shards(): lax.all_gather(jnp.concatenate([attended, activated], 1), 'col', axis=1,...  48.5 us
    psum x1, blocking collectives, shards(): lax.psum((jnp.sum(grad_attn_in * normal, 0), jnp.sum(grad_attn_in, 0), jn...  14.2 us
    psum x1, blocking collectives, shards(): lax.psum((jnp.sum(residual, 1), jnp.sum(residual * residual, 1)), 'col')  12.1 us
    psum x1, blocking collectives, shards(): lax.psum((jnp.sum(grad_normal, 1), jnp.sum(grad_normal * normal, 1)), 'col')  9.68 us
  transfers between devices with their start and end apart: 8, of which 5 were waited for; matrix products, arithmetic and copies ran while one was open for 9% of the time, Pallas kernels for 0%

commit v1 on v0

--- a/solution.py
+++ b/solution.py
@@ -178,8 +178,14 @@
     attended, log_total = attend(queries, keys_b, values, segments)
     attended = attended.reshape(length, att_width).astype(jnp.bfloat16)
     activated = (up_proj * normal_cdf(up_proj)).astype(jnp.bfloat16)
-    mixed_cols = lax.all_gather(
-        jnp.concatenate([attended, activated], 1), "col", axis=1, tiled=True
+    mixed_cols = jnp.concatenate(
+        lax.all_to_all(
+            jnp.stack([jnp.concatenate([attended, activated], 1)] * lax.axis_size("col")),
+            "col",
+            0,
+            0,
+        ),
+        axis=1,
     )
     joined_grid = jnp.concatenate(
         [

time: 465 us -> 470 us (1.011)
  starting transfers between devices: 4.32 us -> 14 us
  waiting for transfers between devices: 312 us -> 303 us
  local copies, waits for them, and re-layouts: 13.2 us -> 18.3 us
    all_gather x1 -> x0, waiting for transfers between devices: 48.5 us -> none  [shards(): lax.all_gather(jnp.concatenate([attended, activated], 1), 'col', axis=1,...]
    all_gather x1, waiting for transfers between devices: 74.6 us -> 119 us  [shards(): first_cols = lax.all_gather(first_back, 'col', axis=1, tiled=True)]
    all_to_all x0 -> x1, starting transfers between devices: none -> 9.76 us  [shards(): lax.all_to_all(jnp.stack([jnp.concatenate([attended, activated], 1)] * la...]
  transfers between devices with their start and end apart: 8 -> 8, of which waited for: 5 -> 4; matrix products, arithmetic and copies ran while one was open for 9% -> 10% of each run, Pallas kernels for 0% -> 0%
where the time goes in v1:
time: 470 us; the launch traced here: 469 us
  waiting for transfers between devices  303 us (64%)
  blocking collectives  59 us (13%)
  other arithmetic  30.3 us (6%)
  matrix products  29.9 us (6%)
  local copies, waits for them, and re-layouts  18.3 us (4%)
  between operations  14.9 us (3%)
  starting transfers between devices  14 us (3%)
    all_gather x1, waiting for transfers between devices, shards(): first_cols = lax.all_gather(first_back, 'col', axis=1, tiled=True)  119 us
    reduce_scatter x1, waiting for transfers between devices, shards(): lax.psum_scatter(jnp.concatenate(blocks, 0), 'col', scatter_dimension=0,...  69.2 us
    all_to_all x1, waiting for transfers between devices, shards(): lax.all_to_all(joined_grid, 'col', split_axis=0, concat_axis=2, tiled=True)  65.1 us
    psum x1, waiting for transfers between devices, shards(): lax.psum(grad_qkv_w.astype(jnp.bfloat16), 'dp').astype(jnp.float32)  49.3 us
    psum x1, blocking collectives, shards(): lax.psum((jnp.sum(grad_attn_in * normal, 0), jnp.sum(grad_attn_in, 0), jn...  13.2 us
    psum x1, blocking collectives, shards(): lax.psum((jnp.sum(residual, 1), jnp.sum(residual * residual, 1)), 'col')  12.1 us
    psum x1, blocking collectives, shards(): lax.psum((jnp.sum(grad_normal, 1), jnp.sum(grad_normal * normal, 1)), 'col')  10.6 us
    all_to_all x1, starting transfers between devices, shards(): lax.all_to_all(jnp.stack([jnp.concatenate([attended, activated], 1)] * la...  9.76 us
  transfers between devices with their start and end apart: 8, of which 4 were waited for; matrix products, arithmetic and copies ran while one was open for 10% of the time, Pallas kernels for 0%

profile of v1, /device:TPU:0, one launch (start us, length us, event | category | flops | bytes accessed | tf_op | source)
XLA Modules:
  0.0 469.3 jit_solution(7831227692561734413)
XLA Ops:
  7.2 9.1 %all_gather.13 = bf16[512,256]{1,0:T(8,128)(2,1)} all-gather(bf16[256,256]{1,0:T(8,128)(2,1)} %param.17), channel_id=1, replica_groups=mesh['dp'=4,'row'=2,'col'=4] {'row'}, dimensions={0}, use_global_device_ids=true | all-gather | bytes 393216 | tf_op jit(solution)/shard_map/all_gather | solution.py:205
  16.4 1.1 convert_reduce_fusion
  17.5 12.1 %all-reduce.2 = (f32[256]{0:T(256)S(1)}, f32[256]{0:T(256)S(1)}) all-reduce(f32[256]{0:T(256)S(1)} %get-tuple-element.74, f32[256]{0:T(256)S(1)} %get-tuple-element.73), channel_id=1, replica_groups=mesh['dp'=4,'row'=2,'col'=4] {'col'}, use_global_device_ids=true, to_apply=%region_3.0 | all-reduce | flops 512 | bytes 4096 | tf_op jit(solution)/shard_map/psum | solution.py:146
  29.6 1.1 fusion.76
  30.7 7.2 %all_gather.12 = bf16[2,512,256]{2,1,0:T(8,128)(2,1)S(1)} all-gather(bf16[2,256,256]{2,1,0:T(8,128)(2,1)S(1)} %pad_maximum_fusion.5), channel_id=1, replica_groups=mesh['dp'=4,'row'=2,'col'=4] {'row'}, dimensions={1}, use_global_device_ids=true | all-gather | bytes 786432 | tf_op jit(solution)/shard_map/all_gather | solution.py:154
  38.5 0.3 fusion.70
  38.9 0.4 fusion.58
  39.5 0.4 fusion.60
  39.9 0.4 fusion.62
  40.2 0.4 fusion.64
  40.6 8.7 %maximum_maximum_fusion = f32[2048,896]{0,1:T(8,128)} fusion(f32[512,512]{0,1:T(8,128)S(1)} %fusion.58, f32[512,384]{0,1:T(8,128)S(1)} %fusion.66, f32[512,512]{0,1:T(8,128)S(1)} %fusion.60, f32[512,384]{0,1:T(8,128)S(1)} %fusion.68, f32[512,512]{0,1:T(8,128)S(1)} %fusion.62, f32[512,384]{0,1:T(8,128)S(1)} %fusion.70, f32[512,512]{0,1:T(8,128)S(1)} %fusion.64, ...), kind=kLoop, calls=%fused_computation.1 | loop fusion | flops 12845056 | bytes 14680064 | tf_op jit(solution)/shard_map/concatenate | solution.py:170
  49.3 1.2 copy-done.14
  50.5 1.1 pad_maximum_fusion
  51.7 3.6 all-to-all-start.1
  55.8 0.9 fusion.33
  56.7 65.1 %all-to-all-done.1 = bf16[4,640,256]{2,1,0:T(8,128)(2,1)S(1)} async-done(((bf16[4,640,256]{2,1,0:T(8,128)(2,1)}), bf16[4,640,256]{2,1,0:T(8,128)(2,1)S(1)}, u32[]{:S(2)}, u32[]{:S(2)}) %all-to-all-start.1) | async-done | bytes 1310752 | tf_op jit(solution)/shard_map/all_to_all | solution.py:211
  121.8 0.7 copy.55
  122.5 2.2 convolution_bitcast_fusion
  124.7 1.0 copy-done.11
  125.8 69.2 %reduce-scatter.4.cloned.1.call-done = f32[512,896]{0,1:T(8,128)} async-done(((f32[2048,896]{0,1:T(8,128)}), f32[512,896]{0,1:T(8,128)}) %reduce-scatter.4.cloned.1.call-update) | async-done | bytes 1835024 | tf_op jit(solution)/shard_map/reduce_scatter | solution.py:170
  195.0 1.2 slice_add_fusion.1
  196.6 0.6 fusion.102
  197.6 1.0 log_add_fusion
  198.6 0.5 fusion.81
  199.1 4.7 fusion.18
  203.7 4.7 fusion.21
  208.4 1.0 slice_multiply_fusion.3
  209.4 2.2 convolution_bitcast_fusion.2
  211.8 0.5 copy-done.16
  212.6 0.6 copy-done.6
  213.3 0.5 copy-done.12
  213.8 0.7 fusion.96
  214.5 1.0 pad_maximum_fusion.1
  215.5 2.1 convolution_convert_fusion.4
  217.9 1.7 stack.46
  219.6 9.8 %all-to-all-start = ((bf16[4,512,640]{2,1,0:T(8,128)(2,1)}), bf16[4,512,640]{2,1,0:T(8,128)(2,1)S(1)}, u32[]{:S(2)}, u32[]{:S(2)}) async-start(bf16[4,512,640]{2,1,0:T(8,128)(2,1)} %stack.46), calls=%async_computation.1 | async-start | bytes 5242880 | tf_op jit(solution)/shard_map/all_to_all | solution.py:182
  229.4 119.0 %all-gather.5.cloned.1.call-done = bf16[512,3584]{0,1:T(8,128)(2,1)} async-done(((bf16[512,896]{0,1:T(8,128)(2,1)}), bf16[512,3584]{0,1:T(8,128)(2,1)}) %all-gather.5.cloned.1.call-update) | async-done | bytes 3670032 | tf_op jit(solution)/shard_map/all_gather | solution.py:227
  348.4 1.7 slice.176
  350.2 2.3 slice.175
  352.5 0.6 fusion.17
  353.2 1.1 copy-done.19
  354.3 0.8 fusion.24
  355.1 0.8 pad_maximum_fusion.4
  356.2 2.7 copy.61
  358.9 2.6 fusion.13
  361.5 1.0 slice.180
  362.5 0.7 slice.179
  363.2 1.6 fusion.16
  364.9 3.1 convolution_convert_fusion.1
  368.0 1.7 convolution_convert_fusion
  369.9 0.8 copy-done.5
  371.0 6.9 %all-reduce.3 = (bf16[384]{0:T(512)(128)(2,1)S(1)}, bf16[256]{0:T(256)(128)(2,1)S(1)}, bf16[512]{0:T(512)(128)(2,1)S(1)}) all-reduce(bf16[384]{0:T(512)(128)(2,1)S(1)} %convert_element_type.134, bf16[256]{0:T(256)(128)(2,1)S(1)} %reduce_sum.129, bf16[512]{0:T(512)(128)(2,1)S(1)} %get-tuple-element.90), channel_id=1, replica_groups=mesh['dp'=4,'row'=2,'col'=4] {'dp'}, use_global_device_ids=true, to_apply=%region_16.17 | all-reduce | flops 1152 | bytes 4608 | tf_op jit(solution)/shard_map/psum | solution.py:264
  377.9 0.6 convert_element_type.135
  378.5 0.6 convert_element_type.142
  379.1 1.0 convert_element_type.129
  380.4 13.2 %all-reduce = (f32[256]{0:T(256)}, f32[256]{0:T(256)}, f32[256]{0:T(256)}, f32[256]{0:T(256)}) all-reduce(f32[256]{0:T(256)S(1)} %get-tuple-element.71, f32[256]{0:T(256)S(1)} %get-tuple-element.68, f32[256]{0:T(256)S(1)} %get-tuple-element.72, f32[256]{0:T(256)S(1)} %get-tuple-element.57), channel_id=1, replica_groups=mesh['dp'=4,'row'=2,'col'=4] {'dp','row'}, use_global_device_ids=true, to_apply=%region_25.26 | all-reduce | flops 1024 | bytes 8192 | tf_op jit(solution)/shard_map/psum | solution.py:253
  393.6 10.6 %all-reduce.1 = (f32[256]{0:T(256)S(1)}, f32[256]{0:T(256)S(1)}) all-reduce(f32[256]{0:T(256)S(1)} %get-tuple-element.70, f32[256]{0:T(256)S(1)} %get-tuple-element.69), channel_id=1, replica_groups=mesh['dp'=4,'row'=2,'col'=4] {'col'}, use_global_device_ids=true, to_apply=%region_13.14 | all-reduce | flops 512 | bytes 4096 | tf_op jit(solution)/shard_map/psum | solution.py:249
  404.2 1.8 fusion.51
  406.0 49.3 %all-reduce.7.cloned.1.call-done = (bf16[256,1536]{1,0:T(8,128)(2,1)}, bf16[512,256]{1,0:T(8,128)(2,1)}, bf16[256,2048]{1,0:T(8,128)(2,1)}, bf16[2048,256]{1,0:T(8,128)(2,1)}) async-done(((bf16[256,1536]{1,0:T(8,128)(2,1)}, bf16[512,256]{1,0:T(8,128)(2,1)}, bf16[256,2048]{1,0:T(8,128)(2,1)}, bf16[2048,256]{1,0:T(8,128)(2,1)}), (bf16[256,1536]{1,0:T(8,128)(2,1)}, bf16[512,256]{1,0:T(8,128)(2,1)}, ...) | async-done | bytes 3145744 | tf_op jit(solution)/shard_map/psum | solution.py:263
  455.4 2.9 convert_element_type.140
  458.2 1.5 convert_element_type.144
  459.7 1.3 convert_element_type.132
  461.1 0.8 convert_element_type.137
  461.9 0.6 copy.81
  (141 shorter events, 4.2 us)
Async XLA Ops:
  7.2 30.7 %copy-start.20 = (bf16[256,1536]{1,0:T(8,128)(2,1)S(1)}, bf16[256,1536]{1,0:T(8,128)(2,1)}, u32[]{:S(2)}) copy-start(bf16[256,1536]{1,0:T(8,128)(2,1)} %param.24) | copy-start | bytes 2359300
  7.2 115.3 %all-gather.3.cloned.1.call-start = ((), (), s32[]{:S(2)}) async-start(), calls=%async_computation.7 | async-start | bytes 1310720 | tf_op jit(solution)/shard_map/all_gather | solution.py:212
  16.4 178.6 %reduce-scatter.4.cloned.1.call-start = ((), (), s32[]{:S(2)}) async-start(), calls=%async_computation.5 | async-start | bytes 9175040 | tf_op jit(solution)/shard_map/reduce_scatter | solution.py:170
  30.7 8.1 %copy-start.18 = (bf16[256,2048]{1,0:T(8,128)(2,1)S(1)}, bf16[256,2048]{1,0:T(8,128)(2,1)}, u32[]{:S(2)}) copy-start(bf16[256,2048]{1,0:T(8,128)(2,1)} %param.28) | copy-start | bytes 3145732
  49.3 1.2 copy-start.14
  49.3 1.3 copy-start.29
  50.5 5.0 %copy-start.42 = (s32[512]{0:T(512)S(1)}, s32[512]{0:T(512)}, u32[]{:S(2)}) copy-start(s32[512]{0:T(512)} %param.19) | copy-start | bytes 6148
  50.5 5.2 %copy-start.37 = (s32[512]{0:T(512)S(1)}, s32[512]{0:T(512)}, u32[]{:S(2)}) copy-start(s32[512]{0:T(512)} %param.18) | copy-start | bytes 6148
  51.7 70.1 %all-to-all-start.1 = ((bf16[4,640,256]{2,1,0:T(8,128)(2,1)}), bf16[4,640,256]{2,1,0:T(8,128)(2,1)S(1)}, u32[]{:S(2)}, u32[]{:S(2)}) async-start(bf16[4,640,256]{2,1,0:T(8,128)(2,1)} %pad_maximum_fusion), calls=%async_computation.3 | async-start | bytes 2621440 | tf_op jit(solution)/shard_map/all_to_all | solution.py:211
  55.3 293.1 %all-gather.5.cloned.1.call-start = ((), (), s32[]{:S(2)}) async-start(), calls=%async_computation.8 | async-start | bytes 4587520 | tf_op jit(solution)/shard_map/all_gather | solution.py:227
  55.7 140.7 %copy-start.26 = (f32[512,16]{0,1:T(8,128)}, f32[512,16]{0,1:T(8,128)S(1)}, u32[]{:S(2)}) copy-start(f32[512,16]{0,1:T(8,128)S(1)} %get-tuple-element.123) | copy-start | bytes 98308
  55.8 140.7 %copy-start.27 = (f32[512,16]{0,1:T(8,128)}, f32[512,16]{0,1:T(8,128)S(1)}, u32[]{:S(2)}) copy-start(f32[512,16]{0,1:T(8,128)S(1)} %get-tuple-element.122) | copy-start | bytes 98308
  122.5 72.5 %copy-start.40 = (f32[384]{0:T(512)S(1)}, f32[384]{0:T(512)}, u32[]{:S(2)}) copy-start(f32[384]{0:T(512)} %param.25) | copy-start | bytes 4612
  124.7 1.1 copy-start.11
  125.8 70.8 %copy-start.32 = (pred[512,512]{0,1:T(8,128)(4,1)S(1)}, pred[512,512]{0,1:T(8,128)(4,1)}, u32[]{:S(2)}) copy-start(pred[512,512]{0,1:T(8,128)(4,1)} %fusion.33) | copy-start | bytes 786436
  196.4 1.1 copy-start.33
  196.5 1.1 copy-start.34
  196.5 1.0 copy-start.35
  196.6 1.0 copy-start.36
  197.2 1.4 copy-start.9
  208.4 3.3 copy-start.22
  208.4 3.3 copy-start.23
  208.4 3.3 copy-start.28
  208.4 3.3 slice-start
  209.4 2.4 slice-start.1
  211.6 0.7 copy-start.16
  211.6 1.7 copy-start.10
  211.6 2.1 copy-start.12
  211.6 2.1 copy-start.41
  211.8 0.7 copy-start.4
  212.5 0.7 copy-start.6
  219.6 136.6 %all-to-all-start = ((bf16[4,512,640]{2,1,0:T(8,128)(2,1)}), bf16[4,512,640]{2,1,0:T(8,128)(2,1)S(1)}, u32[]{:S(2)}, u32[]{:S(2)}) async-start(bf16[4,512,640]{2,1,0:T(8,128)(2,1)} %stack.46), calls=%async_computation.1 | async-start | bytes 5242880 | tf_op jit(solution)/shard_map/all_to_all | solution.py:182
  229.4 149.7 %reduce-scatter.8.cloned.1.call-start = ((), (), s32[]{:S(2)}) async-start(), calls=%async_computation.9 | async-start | bytes 786432 | tf_op jit(solution)/shard_map/reduce_scatter | solution.py:234
  350.2 3.0 copy-start
  350.2 2.4 copy-start.21
  352.5 2.6 copy-start.2
  352.5 1.8 copy-start.19
  355.9 48.3 %reduce-scatter.6.cloned.1.call-start = ((), (), s32[]{:S(2)}) async-start(), calls=%async_computation.6 | async-start | bytes 393216 | tf_op jit(solution)/shard_map/reduce_scatter | solution.py:198
  356.2 2.7 copy-start.3
  361.5 1.8 copy-start.15
  361.5 1.8 copy-start.30
  364.8 3.2 copy-start.1
  364.8 90.5 %all-reduce.7.cloned.1.call-start = ((), (), s32[]{:S(2)}) async-start(), calls=%async_computation.10 | async-start | bytes 6291456 | tf_op jit(solution)/shard_map/psum | solution.py:263
  369.7 1.0 copy-start.5
  369.7 1.0 copy-start.7
  369.7 1.1 copy-start.17
  369.7 10.4 %copy-start.8 = (bf16[256,256]{1,0:T(8,128)(2,1)S(1)}, bf16[256,256]{1,0:T(8,128)(2,1)}, u32[]{:S(2)}) copy-start(bf16[256,256]{1,0:T(8,128)(2,1)} %param.16) | copy-start | bytes 393220
  369.7 10.4 %copy-start.38 = (f32[256]{0:T(256)S(1)}, f32[256]{0:T(256)}, u32[]{:S(2)}) copy-start(f32[256]{0:T(256)} %param.20) | copy-start | bytes 3076
  369.7 10.4 %copy-start.39 = (f32[256]{0:T(256)S(1)}, f32[256]{0:T(256)}, u32[]{:S(2)}) copy-start(f32[256]{0:T(256)} %param.22) | copy-start | bytes 3076
  369.8 34.4 %copy-start.25 = (bf16[256,256]{1,0:T(8,128)(2,1)S(1)}, bf16[256,256]{1,0:T(8,128)(2,1)}, u32[]{:S(2)}) copy-start(bf16[256,256]{1,0:T(8,128)(2,1)} %param.17) | copy-start | bytes 393220
  369.8 34.4 %copy-start.43 = (f32[256]{0:T(256)S(1)}, f32[256]{0:T(256)}, u32[]{:S(2)}) copy-start(f32[256]{0:T(256)} %param.31) | copy-start | bytes 3076
  369.8 34.4 %copy-start.44 = (f32[256]{0:T(256)S(1)}, f32[256]{0:T(256)}, u32[]{:S(2)}) copy-start(f32[256]{0:T(256)} %param.27) | copy-start | bytes 3076
  379.1 82.8 %copy-start.45 = (f32[256]{0:T(256)}, f32[256]{0:T(256)S(1)}, u32[]{:S(2)}) copy-start(f32[256]{0:T(256)S(1)} %convert_element_type.138) | copy-start | bytes 3076
  455.4 2.9 copy-start.13
  458.2 1.5 copy-start.24
  458.2 2.8 copy-start.31
Sparse Core Ops, SparseCore 0:
  16.5 30.1 all-gather.2
  49.4 145.5 reduce-scatter.3
  215.6 132.7 all-gather.4
  356.1 13.7 reduce-scatter.7
  371.9 11.7 reduce-scatter.5
  386.7 68.5 all-reduce.6
